TPU v7x, 32 devices: a whole 2x2x4 slice. The times are simulated.
32 devices in a mesh: doc: 4 (over z), feat: 8 (over y, x, core).
Axes of the slice: x: 2, y: 2, z: 4, core: 2. Of those that a mesh axis runs over, the one named last changes fastest.
Arguments:
- documents: bfloat16 [512, 512], P('doc', 'feat'), may hold values from -6 to 6
- directions: bfloat16 [512, 32768], P('doc', 'feat'), may hold values from -0.5 to 0.5
- phase: float32 [32768], P('feat'), may hold values from -3.140625 to 3.140625
- amplitude: float32 [32768], P('feat'), may hold values from 0.4 to 2.3
- doc_weight: float32 [512], P('doc'), may hold values from 0.5 to 4.2
- labels: int32 [512], P('doc'), may hold values from 0 to 127
Outputs:
- margins: float32 [512, 128], P('doc')
- scaled_weights: float32 [32768, 128], P('feat')
All inputs are finite; a program needn't handle non-finite values.
Results may differ from a plain program's by a relative error of at most 0.0003.
Values may be sent and summed in bfloat16 or wider, within the bound.
A program may use at most 64 MiB of HBM per device.

v0:
```python
import jax
import jax.numpy as jnp
from jax import lax
from jax.sharding import PartitionSpec as P

C = 128
ITERS = 3
NEWTON = 3


shrink_level = 0.1
ratio_floor = 1e-06


def project_tile(features, factor, start, target):
    residue = target - jnp.dot(features, start, precision=lax.Precision.HIGHEST)
    halfway = lax.linalg.triangular_solve(factor, residue, left_side=True, lower=True)
    solved = lax.linalg.triangular_solve(
        factor, halfway, left_side=True, lower=True, transpose_a=True
    )
    new_copy = start + lax.dot_general(
        features, solved, (((0,), (0,)), ((), ())), precision=lax.Precision.HIGHEST
    )
    new_part = jnp.dot(features, new_copy, precision=lax.Precision.HIGHEST)
    return (new_copy, new_part)


def logistic_prox(target, signs, weight_ratio):
    current = target
    for newton_step in range(NEWTON):
        chance = jax.nn.sigmoid(-signs * current)
        gradient = current - target - weight_ratio * signs * chance
        current = current - gradient / (1.0 + weight_ratio * chance * (1.0 - chance))
    return current


def shrink_values(target, limit):
    return target - jnp.clip(target, -limit, limit)


def per_device(documents, directions, phase, amplitude, doc_weight, labels):
    doc_full = lax.all_gather(documents, "feat", axis=1, tiled=True)
    doc_count = documents.shape[0]
    width_tile = directions.shape[1]
    num_feat = lax.axis_size("feat")
    num_doc = lax.axis_size("doc")
    angles = jnp.dot(
        doc_full,
        lax.all_gather(directions, "doc", axis=0, tiled=True),
        preferred_element_type=jnp.float32,
    )
    features = jnp.sqrt(2.0 / width_tile) * amplitude * jnp.cos(angles + phase)
    gram = jnp.eye(doc_count, dtype=jnp.float32) + lax.dot_general(
        features, features, (((1,), (1,)), ((), ())), precision=lax.Precision.HIGHEST
    )
    factor = jnp.linalg.cholesky(gram)
    signs = jnp.where(labels[:, None] == jnp.arange(C, dtype=jnp.int32)[None, :], 1.0, -1.0).astype(
        jnp.float32
    )
    share_rows = doc_count // num_feat
    offset = lax.axis_index("feat") * share_rows
    local_signs = lax.dynamic_slice_in_dim(signs, offset, share_rows, 0)
    local_weight = lax.dynamic_slice_in_dim(doc_weight, offset, share_rows, 0)[:, None]
    rho = jnp.float32(1.0)
    margins = logistic_prox(
        jnp.zeros(local_signs.shape, jnp.float32), local_signs, local_weight / rho
    )
    sums = jnp.zeros(local_signs.shape, jnp.float32)
    duals_y = jnp.zeros(local_signs.shape, jnp.float32)
    duals_x = jnp.zeros((width_tile, C), jnp.float32)
    partial_value = jnp.zeros((doc_count, C), jnp.float32)
    weights = jnp.zeros((width_tile, C), jnp.float32)
    for step in range(ITERS):
        correction = (margins - duals_y - sums) / num_feat
        correction = lax.all_gather(correction, "feat", axis=0, tiled=True)
        new_copy, partial_value = project_tile(
            features, factor, weights - duals_x, partial_value + correction
        )
        sums = lax.psum_scatter(partial_value, "feat", scatter_dimension=0, tiled=True)
        old_weights = weights
        old_margins = margins
        limit = shrink_level / (rho * num_doc)
        summed = lax.psum(new_copy + duals_x, "doc")
        weights = shrink_values(summed / num_doc, limit)
        margins = logistic_prox(sums + duals_y, local_signs, local_weight / rho)
        duals_x = duals_x + new_copy - weights
        duals_y = duals_y + sums - margins
        if step + 1 < ITERS:
            margin_gap = jnp.sum((sums - margins) ** 2)
            margin_move = jnp.sum((margins - old_margins) ** 2)
            primal, dual_norm = lax.psum(
                (
                    jnp.sum((new_copy - weights) ** 2) + margin_gap,
                    jnp.sum((weights - old_weights) ** 2) + margin_move,
                ),
                ("doc", "feat"),
            )
            dual_norm = rho * rho * dual_norm
            growth = ((primal + ratio_floor) / (dual_norm + ratio_floor)) ** 0.25
            rho = rho * growth
            duals_x = duals_x / growth
            duals_y = duals_y / growth
    margins = lax.all_gather(margins, "feat", axis=0, tiled=True)
    return (margins, num_feat * weights)


def solution(mesh):
    in_specs = (P("doc", "feat"), P("doc", "feat"), P("feat"), P("feat"), P("doc"), P("doc"))
    out_specs = (P("doc", None), P("feat", None))
    return jax.shard_map(
        per_device, mesh=mesh, in_specs=in_specs, out_specs=out_specs, check_vma=False
    )
```

profile of v0, /device:TPU:0, one launch (start us, length us, event | category | flops | bytes accessed | tf_op | source)
XLA Modules:
  0.0 657.2 jit_solution(7295771002411407596)
XLA Ops:
  7.2 0.0 all-gather.2.cloned.1.call-start
  7.2 0.7 all-gather.2.cloned.1.call-update
  7.9 0.0 reduce-scatter.4.cloned.1.call-start
  7.9 0.7 dynamic-slice
  8.7 0.7 dynamic_slice.6
  9.4 0.1 broadcast_multiply_fusion.1
  9.6 10.7 %all_gather.20 = f32[128,128]{1,0:T(8,128)S(1)} all-gather(f32[16,128]{1,0:T(8,128)S(1)} %broadcast_multiply_fusion.1), channel_id=1, replica_groups=mesh['doc'=4,'feat'=8] {'feat'}, dimensions={0}, use_global_device_ids=true | all-gather | bytes 73728 | tf_op jit(solution)/shard_map/all_gather | solution.py:75
  20.3 9.2 %all_gather.18 = bf16[128,512]{0,1:T(8,128)(2,1)S(1)} all-gather(bf16[128,64]{0,1:T(8,128)(2,1)} %param.10), channel_id=1, replica_groups=mesh['doc'=4,'feat'=8] {'feat'}, dimensions={1}, use_global_device_ids=true | all-gather | bytes 147456 | tf_op jit(solution)/shard_map/all_gather | solution.py:42
  29.5 0.7 broadcast_multiply_fusion
  30.2 62.9 %all-gather.2.cloned.1.call-done = bf16[512,4096]{1,0:T(8,128)(2,1)} async-done(((bf16[128,4096]{1,0:T(8,128)(2,1)}), bf16[512,4096]{1,0:T(8,128)(2,1)}) %all-gather.2.cloned.1.call-update) | async-done | bytes 4194320 | tf_op jit(solution)/shard_map/all_gather | solution.py:49
  93.0 9.3 %fusion.1 = f32[128,4096]{1,0:T(8,128)S(1)} fusion(bf16[128,512]{0,1:T(8,128)(2,1)S(1)} %all_gather.18, bf16[512,4096]{1,0:T(8,128)(2,1)} %all-gather.2.cloned.1.call-done, f32[4096]{0:T(1024)} %param.12, f32[4096]{0:T(1024)S(1)} %broadcast_multiply_fusion), kind=kOutput, calls=%fused_computation.4 | convolution fusion | flops 537919488 | bytes 6455296 | tf_op jit(solution)/shard_map/dot_general | solution.py:47
  102.3 1.8 fusion.140
  104.1 1.8 convolution_subtract_fusion.2
  105.9 0.1 copy.8
  106.0 11.7 %cholesky.20 = f32[128,128]{1,0:T(8,128)S(1)} custom-call(f32[128,128]{1,0:T(8,128)S(1)} %fusion.22), custom_call_target="Cholesky" | custom-call | tf_op jit(solution)/shard_map/jit(cholesky)/cholesky | solution.py:56
  117.8 0.6 compare_reduce_fusion
  118.4 0.7 fusion.8
  119.1 9.8 %custom-call.14 = f32[1,128,128]{1,2,0:T(8,128)S(1)} custom-call(f32[1,128,128]{2,1,0:T(8,128)S(1)} %fusion.8), custom_call_target="InvertDiagBlocksLowerTriangular" | custom-call | tf_op jit(solution)/shard_map/triangular_solve/custom-call.2 | solution.py:18
  128.9 0.3 fusion.17
  129.2 0.2 fusion.19
  129.4 5.2 fusion.141
  134.6 4.4 fusion.142
  138.9 0.0 reduce-scatter.4.cloned.1.call-update
  138.9 0.0 all-reduce.6.cloned.1.call-start
  139.0 0.7 all-reduce.6.cloned.1.call-update
  139.7 0.0 reduce-scatter.6.cloned.1.call-start
  139.7 31.4 %reduce-scatter.4.cloned.1.call-done = f32[16,128]{1,0:T(8,128)} async-done(((f32[128,128]{1,0:T(8,128)}), f32[16,128]{1,0:T(8,128)}) %reduce-scatter.4.cloned.1.call-update) | async-done | bytes 8208 | tf_op jit(solution)/shard_map/reduce_scatter | solution.py:79
  171.1 1.5 multiply_reduce_fusion.6
  172.6 1.4 multiply_reduce_fusion.7
  173.9 86.3 %all-reduce.6.cloned.1.call-done = f32[4096,128]{1,0:T(8,128)} async-done(((f32[4096,128]{1,0:T(8,128)}), f32[4096,128]{1,0:T(8,128)}) %all-reduce.6.cloned.1.call-update) | async-done | bytes 2097168 | tf_op jit(solution)/shard_map/psum | solution.py:83
  260.2 3.4 multiply_reduce_fusion.2
  266.0 39.3 %all-reduce.1 = (f32[]{:T(128)}, f32[]{:T(128)}) all-reduce(f32[]{:T(128)S(6)} %add.189, f32[]{:T(128)S(6)} %add.191), channel_id=1, replica_groups=mesh['doc'=4,'feat'=8] {'doc','feat'}, use_global_device_ids=true, to_apply=%region_6.9 | all-reduce | flops 2 | bytes 16 | tf_op jit(solution)/shard_map/psum | solution.py:91
  306.6 10.2 %all_gather.21 = f32[128,128]{1,0:T(8,128)S(1)} all-gather(f32[16,128]{1,0:T(8,128)S(1)} %subtract_multiply_fusion.2), channel_id=1, replica_groups=mesh['doc'=4,'feat'=8] {'feat'}, dimensions={0}, use_global_device_ids=true | all-gather | bytes 73728 | tf_op jit(solution)/shard_map/all_gather | solution.py:75
  316.8 4.9 convolution_subtract_fusion.1
  321.7 0.3 fusion.13
  322.0 0.2 fusion.15
  322.3 5.1 fusion.5
  327.3 1.3 copy-done.2
  328.7 2.8 fusion.143
  331.5 0.0 reduce-scatter.6.cloned.1.call-update
  331.5 0.0 all-reduce.8.cloned.1.call-start
  331.5 0.5 all-reduce.8.cloned.1.call-update
  332.1 0.0 reduce-scatter.8.cloned.1.call-start
  332.2 0.1 broadcast_divide_fusion.3
  332.3 31.9 %reduce-scatter.6.cloned.1.call-done = f32[16,128]{1,0:T(8,128)} async-done(((f32[128,128]{1,0:T(8,128)}), f32[16,128]{1,0:T(8,128)}) %reduce-scatter.6.cloned.1.call-update) | async-done | bytes 8208 | tf_op jit(solution)/shard_map/reduce_scatter | solution.py:79
  364.2 1.5 multiply_reduce_fusion.4
  365.7 87.4 %all-reduce.8.cloned.1.call-done = f32[4096,128]{1,0:T(8,128)} async-done(((f32[4096,128]{1,0:T(8,128)}), f32[4096,128]{1,0:T(8,128)}) %all-reduce.8.cloned.1.call-update) | async-done | bytes 2097168 | tf_op jit(solution)/shard_map/psum | solution.py:83
  453.1 4.4 multiply_reduce_fusion
  460.0 39.3 %all-reduce = (f32[]{:T(128)}, f32[]{:T(128)}) all-reduce(f32[]{:T(128)S(6)} %add.203, f32[]{:T(128)S(6)} %add.205), channel_id=1, replica_groups=mesh['doc'=4,'feat'=8] {'doc','feat'}, use_global_device_ids=true, to_apply=%region_14.17 | all-reduce | flops 2 | bytes 16 | tf_op jit(solution)/shard_map/psum | solution.py:91
  500.6 10.4 %all_gather.22 = f32[128,128]{1,0:T(8,128)S(1)} all-gather(f32[16,128]{1,0:T(8,128)S(1)} %subtract_multiply_fusion.1), channel_id=1, replica_groups=mesh['doc'=4,'feat'=8] {'feat'}, dimensions={0}, use_global_device_ids=true | all-gather | bytes 73728 | tf_op jit(solution)/shard_map/all_gather | solution.py:75
  511.1 5.0 convolution_subtract_fusion
  516.1 0.3 fusion.9
  516.4 0.2 fusion.11
  516.6 5.1 fusion.6
  521.7 2.8 fusion.144
  524.5 0.0 all-reduce.10.cloned.1.call-start
  524.6 0.7 all-reduce.10.cloned.1.call-update
  525.3 0.1 broadcast_divide_fusion.2
  525.4 31.8 %reduce-scatter.8.cloned.1.call-done = f32[16,128]{1,0:T(8,128)} async-done(((f32[128,128]{1,0:T(8,128)}), f32[16,128]{1,0:T(8,128)}) %reduce-scatter.8.cloned.1.call-update) | async-done | bytes 8208 | tf_op jit(solution)/shard_map/reduce_scatter | solution.py:79
  557.2 0.8 fusion.64
  558.1 9.2 %all_gather.23 = f32[128,128]{1,0:T(8,128)S(1)} all-gather(f32[16,128]{1,0:T(8,128)S(1)} %fusion.64), channel_id=1, replica_groups=mesh['doc'=4,'feat'=8] {'feat'}, dimensions={0}, use_global_device_ids=true | all-gather | bytes 73728 | tf_op jit(solution)/shard_map/all_gather | solution.py:103
  567.3 79.0 %all-reduce.10.cloned.1.call-done = f32[4096,128]{1,0:T(8,128)} async-done(((f32[4096,128]{1,0:T(8,128)}), f32[4096,128]{1,0:T(8,128)}) %all-reduce.10.cloned.1.call-update) | async-done | bytes 2097168 | tf_op jit(solution)/shard_map/psum | solution.py:83
  646.3 3.2 subtract_multiply_fusion
  649.5 0.6 copy.13
  (24 shorter events, 0.1 us)
Async XLA Ops:
  7.2 85.9 %all-gather.2.cloned.1.call-start = ((), (), s32[]{:S(2)}) async-start(), calls=%async_computation.3 | async-start | bytes 5242880 | tf_op jit(solution)/shard_map/all_gather | solution.py:49
  7.9 163.2 %reduce-scatter.4.cloned.1.call-start = ((), (), s32[]{:S(2)}) async-start(), calls=%async_computation.5 | async-start | bytes 73728 | tf_op jit(solution)/shard_map/reduce_scatter | solution.py:79
  138.9 121.3 %all-reduce.6.cloned.1.call-start = ((), (), s32[]{:S(2)}) async-start(), calls=%async_computation.4 | async-start | bytes 4194304 | tf_op jit(solution)/shard_map/psum | solution.py:83
  139.7 224.5 %reduce-scatter.6.cloned.1.call-start = ((), (), s32[]{:S(2)}) async-start(), calls=%async_computation.7 | async-start | bytes 73728 | tf_op jit(solution)/shard_map/reduce_scatter | solution.py:79
  173.9 132.6 %copy-start.8 = (f32[16,128]{1,0:T(8,128)S(1)}, f32[16,128]{1,0:T(8,128)}, u32[]{:S(2)}) copy-start(f32[16,128]{1,0:T(8,128)} %reduce-scatter.4.cloned.1.call-done) | copy-start | bytes 24580
  173.9 142.9 %copy-start.6 = (f32[128,128]{1,0:T(8,128)S(1)}, f32[128,128]{1,0:T(8,128)}, u32[]{:S(2)}) copy-start(f32[128,128]{1,0:T(8,128)} %fusion.142) | copy-start | bytes 196612
  316.8 5.4 copy-start
  316.8 5.4 copy-start.1
  327.3 1.3 copy-start.2
  331.5 0.7 copy-start.9
  331.5 121.6 %all-reduce.8.cloned.1.call-start = ((), (), s32[]{:S(2)}) async-start(), calls=%async_computation.6 | async-start | bytes 4194304 | tf_op jit(solution)/shard_map/psum | solution.py:83
  332.1 225.1 %reduce-scatter.8.cloned.1.call-start = ((), (), s32[]{:S(2)}) async-start(), calls=%async_computation.8 | async-start | bytes 73728 | tf_op jit(solution)/shard_map/reduce_scatter | solution.py:79
  365.7 135.0 %copy-start.7 = (f32[16,128]{1,0:T(8,128)S(1)}, f32[16,128]{1,0:T(8,128)}, u32[]{:S(2)}) copy-start(f32[16,128]{1,0:T(8,128)} %reduce-scatter.6.cloned.1.call-done) | copy-start | bytes 24580
  365.7 145.4 %copy-start.5 = (f32[128,128]{1,0:T(8,128)S(1)}, f32[128,128]{1,0:T(8,128)}, u32[]{:S(2)}) copy-start(f32[128,128]{1,0:T(8,128)} %fusion.143) | copy-start | bytes 196612
  511.1 5.5 copy-start.3
  511.1 5.5 copy-start.4
  524.5 121.8 %all-reduce.10.cloned.1.call-start = ((), (), s32[]{:S(2)}) async-start(), calls=%async_computation.9 | async-start | bytes 4194304 | tf_op jit(solution)/shard_map/psum | solution.py:83
Sparse Core Ops, SparseCore 0:
  9.5 83.4 all-gather.1
  139.1 31.9 reduce-scatter.3
  174.0 86.1 all-reduce.5
  331.6 32.5 reduce-scatter.5
  367.0 86.0 all-reduce.7
  524.6 32.5 reduce-scatter.7
  560.1 86.0 all-reduce.9
where the time goes:
time: 667 us; the launch traced here: 657 us
  waiting for transfers between devices  413 us (62%)
  blocking collectives  128 us (19%)
  matrix products  49.5 us (7%)
  other arithmetic  40.1 us (6%)
  between operations  22.1 us (3%)
    psum x3, waiting for transfers between devices, per_device(): summed = lax.psum(new_copy + duals_x, 'doc')  253 us
    reduce_scatter x3, waiting for transfers between devices, per_device(): lax.psum_scatter(partial_value, 'feat', scatter_dimension=0, tiled=True)  95.1 us
    psum x2, blocking collectives, per_device(): lax.psum((jnp.sum((new_copy - weights) ** 2) + margin_gap, jnp.sum((weigh...  78.6 us
    all_gather x1, waiting for transfers between devices, per_device(): lax.all_gather(directions, 'doc', axis=0, tiled=True)  62.9 us
    all_gather x3, blocking collectives, per_device(): correction = lax.all_gather(correction, 'feat', axis=0, tiled=True)  31.4 us
    dot_general x3, matrix products, project_tile(): lax.dot_general(features, solved, (((0,), (0,)), ((), ())), precision=lax...  15.3 us
  transfers between devices with their start and end apart: 7, of which 7 were waited for; matrix products, arithmetic and copies ran while one was open for 1% of the time, Pallas kernels for 0%

commit v1 on v0

v1 whole, which is shorter than its diff:
```python
import jax
import jax.numpy as jnp
from jax import lax
from jax.sharding import PartitionSpec as P

C = 128
ITERS = 3
NEWTON = 3
HI = lax.Precision.HIGHEST

shrink_level = 0.1
ratio_floor = 1e-06


def logistic_prox(target, signs, weight_ratio):
    current = target
    for newton_step in range(NEWTON):
        chance = jax.nn.sigmoid(-signs * current)
        gradient = current - target - weight_ratio * signs * chance
        current = current - gradient / (1.0 + weight_ratio * chance * (1.0 - chance))
    return current


def shrink_values(target, limit):
    return target - jnp.clip(target, -limit, limit)


def per_device(documents, directions, phase, amplitude, doc_weight, labels):
    doc_count = documents.shape[0]
    width_tile = directions.shape[1]
    num_feat = lax.axis_size("feat")
    num_doc = lax.axis_size("doc")
    chunk = width_tile // num_doc
    row = lax.axis_index("doc")
    doc_rows = lax.all_gather(documents, "feat", axis=1, tiled=True)
    doc_full = lax.all_gather(doc_rows, "doc", axis=0, tiled=True)
    dir_chunk = lax.all_to_all(directions, "doc", split_axis=1, concat_axis=0, tiled=True)
    phase_c = lax.dynamic_slice_in_dim(phase, row * chunk, chunk, 0)
    amp_c = lax.dynamic_slice_in_dim(amplitude, row * chunk, chunk, 0)
    angles = jnp.dot(doc_full, dir_chunk, preferred_element_type=jnp.float32)
    features = jnp.sqrt(2.0 / width_tile) * amp_c * jnp.cos(angles + phase_c)
    blocks = features.reshape(num_doc, doc_count, chunk)
    gram = jnp.einsum("iac,ibc->iab", blocks, blocks, precision=HI)
    gram = lax.psum_scatter(gram, "doc", scatter_dimension=0, tiled=True)[0]
    eye = jnp.eye(doc_count, dtype=jnp.float32)
    factor = jnp.linalg.cholesky(eye + gram)
    lower_inv = lax.linalg.triangular_solve(factor, eye, left_side=True, lower=True)
    inverse = lax.dot_general(lower_inv, lower_inv, (((0,), (0,)), ((), ())), precision=HI)
    signs = jnp.where(labels[:, None] == jnp.arange(C, dtype=jnp.int32)[None, :], 1.0, -1.0).astype(
        jnp.float32
    )
    share_rows = doc_count // num_feat
    offset = lax.axis_index("feat") * share_rows
    signs = lax.dynamic_slice_in_dim(signs, offset, share_rows, 0)
    weight = lax.dynamic_slice_in_dim(doc_weight, offset, share_rows, 0)[:, None]
    rho = jnp.float32(1.0)
    margins = logistic_prox(jnp.zeros(signs.shape, jnp.float32), signs, weight / rho)
    sums = jnp.zeros(signs.shape, jnp.float32)
    duals_y = jnp.zeros(signs.shape, jnp.float32)
    part = jnp.zeros((doc_count, C), jnp.float32)
    image = jnp.zeros((doc_count, C), jnp.float32)
    weights = jnp.zeros((chunk, C), jnp.float32)
    product = jnp.zeros((doc_count, C), jnp.float32)
    for step in range(ITERS):
        correction = (margins - duals_y - sums) / num_feat
        correction = lax.all_gather(correction, "feat", axis=0, tiled=True)
        target = part + correction
        residue = target - image
        solved = jnp.dot(inverse, residue, precision=HI)
        applied = residue - solved
        part = target - solved
        sums = lax.psum_scatter(part, "feat", scatter_dimension=0, tiled=True)
        all_solved = lax.all_gather(solved, "doc", axis=0, tiled=True)
        lifted = lax.dot_general(features, all_solved, (((0,), (0,)), ((), ())), precision=HI)
        old_weights = weights
        old_margins = margins
        weights = shrink_values(weights + lifted / num_doc, shrink_level / (rho * num_doc))
        margins = logistic_prox(sums + duals_y, signs, weight / rho)
        duals_y = duals_y + sums - margins
        if step + 1 < ITERS:
            move = old_weights - weights
            if step == 0:
                d_move, d_solved, d_applied, d_lifted = move, solved, applied, lifted
            else:
                d_move = move - last_move / growth
                d_solved = solved - last_solved / growth
                d_applied = applied - last_applied / growth
                d_lifted = lifted - last_lifted / growth
            primal = (
                jnp.sum(num_doc * d_move * d_move + 2.0 * d_move * d_lifted)
                + jnp.sum(d_solved * d_applied)
                + jnp.sum((sums - margins) ** 2)
            )
            dual = num_doc * jnp.sum(move**2) + jnp.sum((margins - old_margins) ** 2)
            primal, dual = lax.psum((primal, dual), ("doc", "feat"))
            primal = jnp.maximum(primal, 0.0)
            new_product = jnp.dot(features, weights, precision=HI)
            new_product = lax.psum_scatter(new_product, "doc", scatter_dimension=0, tiled=True)
            growth = ((primal + ratio_floor) / (rho * rho * dual + ratio_floor)) ** 0.25
            rho = rho * growth
            duals_y = duals_y / growth
            image = new_product - (product - new_product + applied) / growth
            product = new_product
            last_move, last_solved, last_applied, last_lifted = move, solved, applied, lifted
    margins = lax.all_gather(margins, "feat", axis=0, tiled=True)
    weights = lax.all_gather(num_feat * weights, "doc", axis=0, tiled=True)
    return (margins, weights)


def solution(mesh):
    in_specs = (P("doc", "feat"), P("doc", "feat"), P("feat"), P("feat"), P("doc"), P("doc"))
    out_specs = (P("doc", None), P("feat", None))
    return jax.shard_map(
        per_device, mesh=mesh, in_specs=in_specs, out_specs=out_specs, check_vma=False
    )
```

time: 667 us -> 385 us (0.58); the launches traced: 657 us -> 384 us
  waiting for transfers between devices: 413 us -> 85.3 us
  blocking collectives: 128 us -> 195 us
  matrix products: 49.5 us -> 33.9 us
  other arithmetic: 40.1 us -> 32.9 us
    psum x3 -> x0, waiting for transfers between devices: 253 us -> none  [per_device(): summed = lax.psum(new_copy + duals_x, 'doc')]
    all_gather x1 -> x5, blocking collectives: 9.17 us -> 76.8 us  [the longest x3 42.2 us: per_device(): all_solved = lax.all_gather(solved, 'doc', axis=0, tiled=True)]
    reduce_scatter x3 -> x6, waiting for transfers between devices: 95.1 us -> 47.4 us  [the longest x3 33.2 us: per_device(): sums = lax.psum_scatter(part, 'feat', scatter_dimension=0, tiled=True)]
    all_gather x1, waiting for transfers between devices: 62.9 us -> 37.8 us  [per_device(): weights = lax.all_gather(num_feat * weights, 'doc', axis=0, tiled=True)]
    dot_general x11, matrix products: 48 us -> 33.7 us  [the longest x3 12.5 us: per_device(): lax.dot_general(features, all_solved, (((0,), (0,)), ((), ())), precision...]
    reduce_sum x5 -> x3, other arithmetic: 12.1 us -> 4.24 us  [the longest x2 2.95 us: per_device(): dual = num_doc * jnp.sum(move ** 2) + jnp.sum((margins - old_margins) ** 2)]
  transfers between devices with their start and end apart: 7 -> 8, of which waited for: 7 -> 5; matrix products, arithmetic and copies ran while one was open for 1% -> 7% of each run, Pallas kernels for 0% -> 0%
where the time goes in v1:
time: 385 us; the launch traced here: 384 us
  blocking collectives  195 us (51%)
  waiting for transfers between devices  85.3 us (22%)
  matrix products  33.9 us (9%)
  other arithmetic  32.9 us (9%)
  between operations  23 us (6%)
  local copies, waits for them, and re-layouts  6.75 us (2%)
  starting transfers between devices  6.6 us (2%)
    psum x2, blocking collectives, per_device(): primal, dual = lax.psum((primal, dual), ('doc', 'feat'))  78.7 us
    all_gather x3, blocking collectives, per_device(): all_solved = lax.all_gather(solved, 'doc', axis=0, tiled=True)  42.2 us
    all_gather x1, waiting for transfers between devices, per_device(): weights = lax.all_gather(num_feat * weights, 'doc', axis=0, tiled=True)  37.8 us
    reduce_scatter x3, waiting for transfers between devices, per_device(): sums = lax.psum_scatter(part, 'feat', scatter_dimension=0, tiled=True)  33.2 us
    all_gather x3, blocking collectives, per_device(): correction = lax.all_gather(correction, 'feat', axis=0, tiled=True)  30.8 us
    all_gather x1, blocking collectives, per_device(): doc_full = lax.all_gather(doc_rows, 'doc', axis=0, tiled=True)  25.3 us
    reduce_scatter x1, waiting for transfers between devices, per_device(): gram = lax.psum_scatter(gram, 'doc', scatter_dimension=0, tiled=True)[0]  14.2 us
    dot_general x3, matrix products, per_device(): lax.dot_general(features, all_solved, (((0,), (0,)), ((), ())), precision...  12.5 us
  transfers between devices with their start and end apart: 8, of which 5 were waited for; matrix products, arithmetic and copies ran while one was open for 7% of the time, Pallas kernels for 0%

profile of v1, /device:TPU:0, one launch (start us, length us, event | category | flops | bytes accessed | tf_op | source)
XLA Modules:
  0.0 383.9 jit_solution(2985545460666034803)
XLA Ops:
  7.2 2.3 copy.10
  9.4 6.3 %all-to-all-start = ((bf16[128,4,1024]{0,2,1:T(8,128)(2,1)}), bf16[128,4,1024]{0,2,1:T(8,128)(2,1)S(1)}, u32[]{:S(2)}, u32[]{:S(2)}) async-start(bf16[128,4,1024]{0,2,1:T(8,128)(2,1)} %bitcast), calls=%async_computation | async-start | bytes 2097152 | tf_op jit(solution)/shard_map/all_to_all | solution.py:37
  15.8 9.2 %all_gather.31 = bf16[128,512]{0,1:T(8,128)(2,1)S(1)} all-gather(bf16[128,64]{0,1:T(8,128)(2,1)S(1)} %copy-done.4), channel_id=1, replica_groups=mesh['doc'=4,'feat'=8] {'feat'}, dimensions={1}, use_global_device_ids=true | all-gather | bytes 147456 | tf_op jit(solution)/shard_map/all_gather | solution.py:35
  25.0 0.7 dynamic-slice_multiply_fusion
  25.7 25.3 %all_gather.32 = bf16[512,512]{0,1:T(8,128)(2,1)} all-gather(bf16[128,512]{0,1:T(8,128)(2,1)S(1)} %all_gather.31), channel_id=1, replica_groups=mesh['doc'=4,'feat'=8] {'doc'}, dimensions={0}, use_global_device_ids=true | all-gather | bytes 655360 | tf_op jit(solution)/shard_map/all_gather | solution.py:36
  51.0 0.5 copy.11
  51.6 8.3 %cosine_multiply_fusion = f32[512,1024]{1,0:T(8,128)S(1)} fusion(bf16[512,512]{0,1:T(8,128)(2,1)} %all_gather.32, bf16[512,1024]{1,0:T(8,128)(2,1)S(1)} %bitcast.38, f32[1024]{0:T(1024)S(1)} %dynamic-slice-done, f32[1024]{0:T(1024)S(1)} %dynamic-slice_multiply_fusion), kind=kOutput, calls=%fused_computation | convolution fusion | flops 537919488 | bytes 3678208 | tf_op jit(solution)/shard_map/dot_general | solution.py:40
  59.9 2.8 fusion.142
  62.7 0.0 reduce-scatter.9.cloned.1.call-start
  62.8 0.1 dynamic-slice
  62.9 0.1 dynamic_slice.12
  62.9 0.1 broadcast_multiply_fusion
  63.1 9.4 %all_gather.30 = f32[128,128]{1,0:T(8,128)S(1)} all-gather(f32[16,128]{1,0:T(8,128)S(1)} %broadcast_multiply_fusion), channel_id=1, replica_groups=mesh['doc'=4,'feat'=8] {'feat'}, dimensions={0}, use_global_device_ids=true | all-gather | bytes 73728 | tf_op jit(solution)/shard_map/all_gather | solution.py:66
  72.5 14.2 %reduce-scatter.7.cloned.1.call-done = f32[1,128,128]{2,1,0:T(8,128)} async-done(((f32[4,128,128]{2,1,0:T(8,128)}), f32[1,128,128]{2,1,0:T(8,128)}) %reduce-scatter.7.cloned.1.call-update) | async-done | bytes 65552 | tf_op jit(solution)/shard_map/reduce_scatter | solution.py:44
  86.7 0.9 bitcast_add_fusion.1
  87.5 0.1 copy.12
  87.6 0.9 fusion.13
  88.5 11.7 %cholesky.18 = f32[128,128]{1,0:T(8,128)S(1)} custom-call(f32[128,128]{1,0:T(8,128)S(1)} %fusion.13), custom_call_target="Cholesky" | custom-call | tf_op jit(solution)/shard_map/jit(cholesky)/cholesky | solution.py:46
  100.2 0.6 compare_reduce_fusion
  100.9 0.7 fusion.10
  101.6 9.8 %custom-call.6 = f32[1,128,128]{1,2,0:T(8,128)S(1)} custom-call(f32[1,128,128]{2,1,0:T(8,128)S(1)} %fusion.10), custom_call_target="InvertDiagBlocksLowerTriangular" | custom-call | tf_op jit(solution)/shard_map/triangular_solve | solution.py:47
  111.4 0.3 fusion.11
  111.6 0.3 fusion.143
  111.9 1.5 multiply_reduce_fusion.3
  113.4 0.0 reduce-scatter.9.cloned.1.call-update
  113.5 0.0 reduce-scatter.11.cloned.1.call-start
  113.5 14.1 %all_gather.33 = f32[512,128]{1,0:T(8,128)S(1)} all-gather(f32[128,128]{1,0:T(8,128)S(1)} %get-tuple-element.23), channel_id=1, replica_groups=mesh['doc'=4,'feat'=8] {'doc'}, dimensions={0}, use_global_device_ids=true | all-gather | bytes 327680 | tf_op jit(solution)/shard_map/all_gather | solution.py:73
  127.6 4.1 %multiply_reduce_fusion.1 = (f32[]{:T(128)}, f32[]{:T(128)}, f32[1024,128]{1,0:T(8,128)S(1)}) fusion(f32[512,1024]{1,0:T(8,128)S(1)} %cosine_multiply_fusion, f32[512,128]{1,0:T(8,128)S(1)} %all_gather.33), kind=kOutput, calls=%fused_computation.13 | convolution fusion | flops 806879232 | bytes 2883592 | tf_op jit(solution)/shard_map/dot_general | solution.py:74
  131.7 2.5 fusion.6
  136.1 0.0 reduce-scatter.11.cloned.1.call-update
  136.1 0.0 reduce-scatter.13.cloned.1.call-start
  136.2 9.2 %reduce-scatter.9.cloned.1.call-done = f32[16,128]{1,0:T(8,128)} async-done(((f32[128,128]{1,0:T(8,128)}), f32[16,128]{1,0:T(8,128)}) %reduce-scatter.9.cloned.1.call-update) | async-done | bytes 8208 | tf_op jit(solution)/shard_map/reduce_scatter | solution.py:72
  145.4 1.5 multiply_reduce_fusion.6
  146.8 1.3 multiply_reduce_fusion.7
  149.3 39.3 %all-reduce.1 = (f32[]{:T(128)}, f32[]{:T(128)}) all-reduce(f32[]{:T(128)S(6)} %add.203, f32[]{:T(128)S(6)} %add.205), channel_id=1, replica_groups=mesh['doc'=4,'feat'=8] {'doc','feat'}, use_global_device_ids=true, to_apply=%region_7.8 | all-reduce | flops 2 | bytes 16 | tf_op jit(solution)/shard_map/psum | solution.py:95
  189.9 0.7 subtract_multiply_fusion.2
  190.6 10.2 %all_gather.34 = f32[128,128]{1,0:T(8,128)S(1)} all-gather(f32[16,128]{1,0:T(8,128)S(1)} %subtract_multiply_fusion.2), channel_id=1, replica_groups=mesh['doc'=4,'feat'=8] {'feat'}, dimensions={0}, use_global_device_ids=true | all-gather | bytes 73728 | tf_op jit(solution)/shard_map/all_gather | solution.py:66
  200.8 0.9 subtract_subtract_fusion
  201.7 1.5 multiply_reduce_fusion.2
  203.2 0.0 reduce-scatter.13.cloned.1.call-update
  203.2 0.0 reduce-scatter.15.cloned.1.call-start
  203.2 14.2 %all_gather.35 = f32[512,128]{1,0:T(8,128)S(1)} all-gather(f32[128,128]{1,0:T(8,128)S(1)} %get-tuple-element.25), channel_id=1, replica_groups=mesh['doc'=4,'feat'=8] {'doc'}, dimensions={0}, use_global_device_ids=true | all-gather | bytes 327680 | tf_op jit(solution)/shard_map/all_gather | solution.py:73
  217.4 4.2 %multiply_reduce_fusion = (f32[]{:T(128)}, f32[]{:T(128)}, f32[1024,128]{1,0:T(8,128)S(1)}) fusion(f32[1024,128]{1,0:T(8,128)S(1)} %get-tuple-element.24, f32[]{:T(128)S(6)} %neg.66, f32[]{:T(128)S(6)} %div.199, f32[]{:T(128)S(6)} %pow.6, f32[512,1024]{1,0:T(8,128)S(1)} %cosine_multiply_fusion, f32[512,128]{1,0:T(8,128)S(1)} %all_gather.35), kind=kOutput, calls=%fused_computation.11 | convolution fusion | flops 808189952 | bytes 3407892 | tf_op jit(solution)/shard_map/dot_general | solution.py:74
  221.6 2.5 fusion.137
  224.2 0.0 reduce-scatter.17.cloned.1.call-start
  224.2 0.1 broadcast_divide_fusion.2
  226.1 9.7 %reduce-scatter.13.cloned.1.call-done = f32[16,128]{1,0:T(8,128)} async-done(((f32[128,128]{1,0:T(8,128)}), f32[16,128]{1,0:T(8,128)}) %reduce-scatter.13.cloned.1.call-update) | async-done | bytes 8208 | tf_op jit(solution)/shard_map/reduce_scatter | solution.py:72
  235.9 1.5 multiply_reduce_fusion.4
  238.5 39.4 %all-reduce = (f32[]{:T(128)}, f32[]{:T(128)}) all-reduce(f32[]{:T(128)S(6)} %add.219, f32[]{:T(128)S(6)} %add.221), channel_id=1, replica_groups=mesh['doc'=4,'feat'=8] {'doc','feat'}, use_global_device_ids=true, to_apply=%region_16.17 | all-reduce | flops 2 | bytes 16 | tf_op jit(solution)/shard_map/psum | solution.py:95
  279.2 0.7 subtract_multiply_fusion.1
  279.9 11.2 %all_gather.36 = f32[128,128]{1,0:T(8,128)} all-gather(f32[16,128]{1,0:T(8,128)S(1)} %subtract_multiply_fusion.1), channel_id=1, replica_groups=mesh['doc'=4,'feat'=8] {'feat'}, dimensions={0}, use_global_device_ids=true | all-gather | bytes 73728 | tf_op jit(solution)/shard_map/all_gather | solution.py:66
  291.1 1.8 fusion.140
  292.9 0.0 reduce-scatter.17.cloned.1.call-update
  292.9 0.0 all-gather.2.cloned.1.call-start
  292.9 14.0 %all_gather.38 = f32[512,128]{1,0:T(8,128)S(1)} all-gather(f32[128,128]{1,0:T(8,128)S(1)} %get-tuple-element.28), channel_id=1, replica_groups=mesh['doc'=4,'feat'=8] {'doc'}, dimensions={0}, use_global_device_ids=true | all-gather | bytes 327680 | tf_op jit(solution)/shard_map/all_gather | solution.py:73
  306.9 4.2 %subtract_multiply_fusion = f32[1024,128]{1,0:T(8,128)} fusion(f32[512,1024]{1,0:T(8,128)S(1)} %cosine_multiply_fusion, f32[512,128]{1,0:T(8,128)S(1)} %all_gather.38, f32[]{:T(128)S(6)} %neg.70, f32[]{:T(128)S(6)} %div.220, f32[]{:T(128)S(6)} %neg.66, f32[]{:T(128)S(6)} %div.199, f32[1024,128]{1,0:T(8,128)S(1)} %get-tuple-element.26, ...), kind=kOutput, calls=%fused_computation.10 | convolution fusion | flops 807141376 | bytes 3932176 | tf_op jit(solution)/shard_map/dot_general | solution.py:74
  311.1 0.0 all-gather.2.cloned.1.call-update
  311.2 0.1 broadcast_divide_fusion.1
  311.2 14.3 %reduce-scatter.17.cloned.1.call-done = f32[16,128]{1,0:T(8,128)} async-done(((f32[128,128]{1,0:T(8,128)}), f32[16,128]{1,0:T(8,128)}) %reduce-scatter.17.cloned.1.call-update) | async-done | bytes 8208 | tf_op jit(solution)/shard_map/reduce_scatter | solution.py:72
  325.6 0.8 fusion.63
  326.4 9.2 %all_gather.37 = f32[128,128]{1,0:T(8,128)S(1)} all-gather(f32[16,128]{1,0:T(8,128)S(1)} %fusion.63), channel_id=1, replica_groups=mesh['doc'=4,'feat'=8] {'feat'}, dimensions={0}, use_global_device_ids=true | all-gather | bytes 73728 | tf_op jit(solution)/shard_map/all_gather | solution.py:105
  335.6 37.8 %all-gather.2.cloned.1.call-done = f32[4096,128]{1,0:T(8,128)} async-done(((f32[1024,128]{1,0:T(8,128)}), f32[4096,128]{1,0:T(8,128)}) %all-gather.2.cloned.1.call-update) | async-done | bytes 2097168 | tf_op jit(solution)/shard_map/all_gather | solution.py:106
  373.4 0.6 copy.15
  374.0 3.0 copy.16
  (29 shorter events, 0.1 us)
Async XLA Ops:
  7.2 8.6 %copy-start.4 = (bf16[128,64]{0,1:T(8,128)(2,1)S(1)}, bf16[128,64]{0,1:T(8,128)(2,1)}, u32[]{:S(2)}) copy-start(bf16[128,64]{0,1:T(8,128)(2,1)} %param.6) | copy-start | bytes 49156
  9.4 41.6 %all-to-all-start = ((bf16[128,4,1024]{0,2,1:T(8,128)(2,1)}), bf16[128,4,1024]{0,2,1:T(8,128)(2,1)S(1)}, u32[]{:S(2)}, u32[]{:S(2)}) async-start(bf16[128,4,1024]{0,2,1:T(8,128)(2,1)} %bitcast), calls=%async_computation | async-start | bytes 2097152 | tf_op jit(solution)/shard_map/all_to_all | solution.py:37
  15.8 70.9 %reduce-scatter.7.cloned.1.call-start = ((), (), s32[]{:S(2)}) async-start(), calls=%async_computation.7 | async-start | bytes 327680 | tf_op jit(solution)/shard_map/reduce_scatter | solution.py:44
  15.8 35.8 %dynamic-slice-start = ((f32[4096]{0:T(1024)}, s32[]{:T(128)}), f32[1024]{0:T(1024)S(1)}, s32[]{:S(2)}) async-start(f32[4096]{0:T(1024)} %param.8, s32[]{:T(128)} %select_n.18), calls=%async_computation.14 | async-start | bytes 8704 | tf_op jit(solution)/shard_map/dynamic_slice | solution.py:38
  59.9 2.9 copy-start.9
  59.9 2.9 copy-start.7
  62.7 82.6 %reduce-scatter.9.cloned.1.call-start = ((), (), s32[]{:S(2)}) async-start(), calls=%async_computation.8 | async-start | bytes 73728 | tf_op jit(solution)/shard_map/reduce_scatter | solution.py:72
  62.9 173.0 %copy-start.5 = (s32[16]{0:T(128)}, s32[16]{0:T(128)S(1)}, u32[]{:S(2)}) copy-start(s32[16]{0:T(128)S(1)} %dynamic-slice) | copy-start | bytes 196
  113.5 87.4 %reduce-scatter.11.cloned.1.call-start = ((), (), s32[]{:S(2)}) async-start(), calls=%async_computation.9 | async-start | bytes 327680 | tf_op jit(solution)/shard_map/reduce_scatter | solution.py:98
  131.7 69.2 %copy-start = (f32[128,128]{1,0:T(8,128)S(1)}, f32[128,128]{1,0:T(8,128)}, u32[]{:S(2)}) copy-start(f32[128,128]{1,0:T(8,128)} %get-tuple-element.20) | copy-start | bytes 196612
  136.1 99.8 %reduce-scatter.13.cloned.1.call-start = ((), (), s32[]{:S(2)}) async-start(), calls=%async_computation.10 | async-start | bytes 73728 | tf_op jit(solution)/shard_map/reduce_scatter | solution.py:72
  203.2 87.9 %reduce-scatter.15.cloned.1.call-start = ((), (), s32[]{:S(2)}) async-start(), calls=%async_computation.11 | async-start | bytes 327680 | tf_op jit(solution)/shard_map/reduce_scatter | solution.py:98
  221.6 69.5 %copy-start.1 = (f32[128,128]{1,0:T(8,128)S(1)}, f32[128,128]{1,0:T(8,128)}, u32[]{:S(2)}) copy-start(f32[128,128]{1,0:T(8,128)} %reduce-scatter.11.cloned.1.call-done) | copy-start | bytes 196612
  221.6 69.5 %copy-start.2 = (f32[128,128]{1,0:T(8,128)S(1)}, f32[128,128]{1,0:T(8,128)}, u32[]{:S(2)}) copy-start(f32[128,128]{1,0:T(8,128)} %get-tuple-element.22) | copy-start | bytes 196612
  224.2 101.4 %reduce-scatter.17.cloned.1.call-start = ((), (), s32[]{:S(2)}) async-start(), calls=%async_computation.12 | async-start | bytes 73728 | tf_op jit(solution)/shard_map/reduce_scatter | solution.py:72
  292.9 80.5 %all-gather.2.cloned.1.call-start = ((), (), s32[]{:S(2)}) async-start(), calls=%async_computation.13 | async-start | bytes 2621440 | tf_op jit(solution)/shard_map/all_gather | solution.py:106
  306.9 4.3 %copy-start.8 = (f32[128]{0:T(128)S(1)}, f32[128]{0:T(128)}, u32[]{:S(2)}) copy-start(f32[128]{0:T(128)} %param.10) | copy-start | bytes 1540
  306.9 18.7 %copy-start.3 = (f32[16,128]{1,0:T(8,128)S(1)}, f32[16,128]{1,0:T(8,128)}, u32[]{:S(2)}) copy-start(f32[16,128]{1,0:T(8,128)} %reduce-scatter.13.cloned.1.call-done) | copy-start | bytes 24580
  306.9 18.7 %copy-start.6 = (s32[16]{0:T(128)S(1)}, s32[16]{0:T(128)}, u32[]{:S(2)}) copy-start(s32[16]{0:T(128)} %copy-done.5) | copy-start | bytes 196
Sparse Core Ops, SparseCore 0:
  62.8 23.8 reduce-scatter.6
  113.6 31.7 reduce-scatter.8
  148.2 19.9 reduce-scatter.10
  203.3 32.4 reduce-scatter.12
  238.5 19.9 reduce-scatter.14
  293.0 32.5 reduce-scatter.16
  327.7 45.6 all-gather.1

commit v2 on v0

v2 whole, which is shorter than its diff:
```python
import functools

import jax
import jax.numpy as jnp
from jax import lax
from jax.experimental import pallas as pl
from jax.experimental.pallas import tpu as pltpu
from jax.sharding import PartitionSpec as P

C = 128
ITERS = 3
NEWTON = 3
HI = lax.Precision.HIGHEST
MESH = pl.DeviceIdType.MESH

shrink_level = 0.1
ratio_floor = 1e-06


def logistic_prox(target, signs, weight_ratio):
    current = target
    for newton_step in range(NEWTON):
        chance = 1.0 / (1.0 + jnp.exp(signs * current))
        gradient = current - target - weight_ratio * signs * chance
        current = current - gradient / (1.0 + weight_ratio * chance * (1.0 - chance))
    return current


def shrink_values(target, limit):
    return target - jnp.minimum(jnp.maximum(target, -limit), limit)


def cosine(angle):
    turns = jnp.floor(angle * 0.3183098861837907 + 0.5)
    rest = angle - turns * 3.140625
    rest = rest - turns * 9.67502593994140625e-4
    rest = rest - turns * 1.509957990978376432e-7
    odd = turns - 2.0 * jnp.floor(turns * 0.5)
    sq = rest * rest
    poly = 2.08767569878681e-9
    poly = poly * sq - 2.755731922398589e-7
    poly = poly * sq + 2.48015873015873e-5
    poly = poly * sq - 1.388888888888889e-3
    poly = poly * sq + 4.1666666666666664e-2
    poly = poly * sq - 0.5
    poly = poly * sq + 1.0
    return poly * (1.0 - 2.0 * odd)


def remote(src, dst, send_sem, recv_sem, axis, peer):
    return pltpu.make_async_remote_copy(
        src_ref=src,
        dst_ref=dst,
        send_sem=send_sem,
        recv_sem=recv_sem,
        device_id={axis: peer},
        device_id_type=MESH,
    )


def greet(num_doc, num_feat):
    barrier = pltpu.get_barrier_semaphore()
    for axis, size in (("doc", num_doc), ("feat", num_feat)):
        me = lax.axis_index(axis)
        for k in range(1, size):
            pl.semaphore_signal(
                barrier, inc=1, device_id={axis: lax.rem(me + k, size)}, device_id_type=MESH
            )
    pl.semaphore_wait(barrier, num_doc + num_feat - 2)


class Channel:
    def __init__(self, sems, axis, size):
        self.sems, self.axis, self.size = sems, axis, size
        self.me = lax.axis_index(axis)
        self.pending = []

    def peers(self):
        return [lax.rem(self.me + k, self.size) for k in range(1, self.size)]

    def send(self, slot, peer, src, dst):
        copy = remote(
            src, dst, self.sems.at[0, slot, peer], self.sems.at[1, slot, self.me], self.axis, peer
        )
        copy.start()
        self.pending.append(copy)

    def arrived(self, slot, peer, ref):
        remote(
            ref, ref, self.sems.at[0, slot, peer], self.sems.at[1, slot, peer], self.axis, peer
        ).wait_recv()

    def drain(self):
        for copy in self.pending:
            copy.wait_send()


def build_kernel(
    num_doc, num_feat, subs, scale,
    docs_ref, dir_ref, phase_ref, amp_ref,
    feat_ref, featt_ref, gram_ref,
    dpart, drow, dirs, gsend, grecv, part_sems, row_sems, dir_sems, gram_sems, local_sem,
):
    n = docs_ref.shape[0]
    chunk = dirs.shape[2]
    wide = chunk // subs
    me = lax.axis_index("doc")
    fme = lax.axis_index("feat")
    greet(num_doc, num_feat)
    ch_part = Channel(part_sems, "feat", num_feat)
    ch_row = Channel(row_sems, "doc", num_doc)
    ch_dir = Channel(dir_sems, "doc", num_doc)
    ch_gram = Channel(gram_sems, "doc", num_doc)
    for peer in ch_part.peers():
        ch_part.send(0, peer, docs_ref, dpart.at[fme])
    local = pltpu.make_async_copy(
        dir_ref.at[:, pl.ds(pl.multiple_of(me * chunk, chunk), chunk)], dirs.at[me], local_sem
    )
    local.start()
    for s in range(subs):
        for peer in ch_dir.peers():
            cols = pl.ds(pl.multiple_of(peer * chunk + s * wide, wide), wide)
            ch_dir.send(
                s, peer, dir_ref.at[:, cols], dirs.at[me, :, pl.ds(s * wide, wide)]
            )
    dpart[fme] = docs_ref[...]
    for peer in ch_part.peers():
        ch_part.arrived(0, peer, dpart.at[peer])
    row = jnp.concatenate(
        [dpart[k].astype(jnp.float32) for k in range(num_feat)], axis=1
    ).astype(jnp.bfloat16)
    drow[me] = row
    for peer in ch_row.peers():
        ch_row.send(0, peer, drow.at[me], drow.at[me])
    for peer in ch_row.peers():
        ch_row.arrived(0, peer, drow.at[peer])
    local.wait()
    full = drow[...].reshape(num_doc * n, drow.shape[2])
    phase = phase_ref[me]
    amp = scale * amp_ref[me]
    for s in range(subs):
        cols = slice(s * wide, (s + 1) * wide)
        for peer in ch_dir.peers():
            ch_dir.arrived(s, peer, dirs.at[peer, :, pl.ds(s * wide, wide)])
        piece = dirs[:, :, cols].reshape(full.shape[1], wide)
        angles = jnp.dot(full, piece, preferred_element_type=jnp.float32)
        feats = amp[:, cols] * cosine(angles + phase[:, cols])
        feat_ref[:, cols] = feats
        featt_ref[cols, :] = feats.T
        for i in range(num_doc):
            block = feats[i * n : (i + 1) * n]
            term = lax.dot_general(block, block, (((1,), (1,)), ((), ())), precision=HI)
            if s == 0:
                gsend[i] = term
            else:
                gsend[i] += term
    for peer in ch_gram.peers():
        ch_gram.send(0, peer, gsend.at[peer], grecv.at[me])
    grecv[me] = gsend[me]
    for peer in ch_gram.peers():
        ch_gram.arrived(0, peer, grecv.at[peer])
    total = grecv[0]
    for i in range(1, num_doc):
        total += grecv[i]
    rows = lax.broadcasted_iota(jnp.int32, (n, n), 0)
    cols = lax.broadcasted_iota(jnp.int32, (n, n), 1)
    gram_ref[...] = total + jnp.where(rows == cols, 1.0, 0.0)
    for channel in (ch_part, ch_row, ch_dir, ch_gram):
        channel.drain()


def fold(values):
    return jnp.sum(values.reshape(values.shape[0] // 8, 8, values.shape[1]), axis=0)


def total(values):
    return jnp.sum(jnp.sum(values, axis=0, keepdims=True), axis=1, keepdims=True)


def admm_kernel(
    num_doc, num_feat, subs,
    feat_ref, featt_ref, inv_ref, lab_ref, dw_ref,
    m_ref, w_ref,
    solved, part, yrecv, cbuf, psend, precv, sc1, sc2, z, lastmove, lastlift,
    s_sems, y_sems, c_sems, p_sems, sc1_sems, sc2_sems, w_sems,
):
    n = inv_ref.shape[0]
    chunk = z.shape[0]
    share = n // num_feat
    wide = chunk // subs
    me = lax.axis_index("doc")
    fme = lax.axis_index("feat")
    greet(num_doc, num_feat)
    ch_s = Channel(s_sems, "doc", num_doc)
    ch_y = Channel(y_sems, "feat", num_feat)
    ch_c = Channel(c_sems, "feat", num_feat)
    ch_p = Channel(p_sems, "doc", num_doc)
    ch_1 = Channel(sc1_sems, "doc", num_doc)
    ch_2 = Channel(sc2_sems, "feat", num_feat)
    classes = lax.broadcasted_iota(jnp.int32, (n, C), 1)
    all_signs = jnp.where(lab_ref[...] == classes, 1.0, -1.0)
    start = logistic_prox(jnp.zeros((n, C), jnp.float32), all_signs, dw_ref[...])
    own = pl.ds(pl.multiple_of(fme * share, share), share)
    signs = jnp.where(
        lab_ref[own, :] == lax.broadcasted_iota(jnp.int32, (share, C), 1), 1.0, -1.0
    )
    weight = dw_ref[own, :]
    margins = logistic_prox(jnp.zeros((share, C), jnp.float32), signs, weight)
    duals = jnp.zeros((share, C), jnp.float32)
    rho = jnp.ones((1, 1), jnp.float32)
    inv = inv_ref[...]
    target = start / num_feat
    residue = target
    growth = None

    def my_rows(src, s):
        return pl.ds(pl.multiple_of(src * chunk + s * wide, wide), wide)

    def w_copy(direction, src, s, peer):
        ref = w_ref.at[my_rows(src, s), :]
        return remote(
            ref, ref, w_sems.at[direction, 0, src, s], w_sems.at[direction, 1, src, s], "doc", peer
        )

    for step in range(ITERS):
        last = step + 1 == ITERS
        answer = jnp.dot(inv, residue, precision=HI)
        applied = residue - answer
        new_part = target - answer
        solved[step, me] = answer
        part[step] = new_part
        for peer in ch_s.peers():
            ch_s.send(step, peer, solved.at[step, me], solved.at[step, me])
        for peer in ch_y.peers():
            rows = pl.ds(pl.multiple_of(peer * share, share), share)
            ch_y.send(step, peer, part.at[step, rows, :], yrecv.at[step, fme])
        yrecv[step, fme] = part[step, own, :]
        for peer in ch_y.peers():
            ch_y.arrived(step, peer, yrecv.at[step, peer])
        sums = yrecv[step, 0]
        for k in range(1, num_feat):
            sums += yrecv[step, k]
        old_margins = margins
        margins = logistic_prox(sums + duals, signs, weight / rho)
        duals = duals + sums - margins
        cbuf[step, fme, 0] = margins if last else (margins - sums) / num_feat
        cbuf[step, fme, 1] = duals / num_feat
        for peer in ch_c.peers():
            ch_c.send(step, peer, cbuf.at[step, fme], cbuf.at[step, fme])
        for peer in ch_s.peers():
            ch_s.arrived(step, peer, solved.at[step, peer])
        everything = solved[step].reshape(num_doc * n, C)
        limit = shrink_level / (rho * num_doc)
        if not last:
            gap = fold((sums - margins) ** 2) if share > 8 else (sums - margins) ** 2
            shift = (
                fold((margins - old_margins) ** 2) if share > 8 else (margins - old_margins) ** 2
            )
            if step == 0:
                d_answer, d_applied = answer, applied
            else:
                d_answer = answer - last_answer / growth
                d_applied = applied - last_applied / growth
            primal = gap + fold(d_answer * d_applied)
            dual = shift
        for s in range(subs):
            rows = slice(s * wide, (s + 1) * wide)
            lift = jnp.dot(featt_ref[rows, :], everything, precision=HI)
            if step == 0:
                fresh = shrink_values(lift / num_doc, limit)
                move = -fresh
                d_move, d_lift = move, lift
            else:
                old = z[rows, :]
                fresh = shrink_values(old + lift / num_doc, limit)
                if not last:
                    move = old - fresh
                    d_move = move - lastmove[rows, :] / growth
                    d_lift = lift - lastlift[rows, :] / growth
            if last:
                w_ref[my_rows(me, s), :] = num_feat * fresh

                @pl.when(me + 1 < num_doc)
                def _(s=s):
                    w_copy(0, me, s, me + 1).start()

                @pl.when(me >= 1)
                def _(s=s):
                    w_copy(1, me, s, me - 1).start()
            else:
                z[rows, :] = fresh
                lastmove[rows, :] = move
                lastlift[rows, :] = lift
                primal += fold(num_doc * d_move * d_move + 2.0 * d_move * d_lift)
                dual += num_doc * fold(move * move)
        if last:
            break
        sc1[step, me, 0] = primal
        sc1[step, me, 1] = dual
        for peer in ch_1.peers():
            ch_1.send(step, peer, sc1.at[step, me], sc1.at[step, me])
        weights = z[...]
        for i in range(num_doc):
            psend[step, i] = jnp.dot(feat_ref[i * n : (i + 1) * n, :], weights, precision=HI)
        for peer in ch_p.peers():
            ch_p.send(step, peer, psend.at[step, peer], precv.at[step, me])
        precv[step, me] = psend[step, me]
        for peer in ch_1.peers():
            ch_1.arrived(step, peer, sc1.at[step, peer])
        both = sc1[step, 0]
        for i in range(1, num_doc):
            both += sc1[step, i]
        sc2[step, fme] = both
        for peer in ch_2.peers():
            ch_2.send(step, peer, sc2.at[step, fme], sc2.at[step, fme])
        for peer in ch_2.peers():
            ch_2.arrived(step, peer, sc2.at[step, peer])
        both = sc2[step, 0]
        for k in range(1, num_feat):
            both += sc2[step, k]
        primal = jnp.maximum(total(both[0]), 0.0)
        dual = total(both[1])
        last_answer, last_applied = answer, applied
        for peer in ch_c.peers():
            ch_c.arrived(step, peer, cbuf.at[step, peer])
        growth = jnp.sqrt(
            jnp.sqrt((primal + ratio_floor) / (rho * rho * dual + ratio_floor))
        )
        rho = rho * growth
        duals = duals / growth
        fixed = cbuf[step, :, 0].reshape(n, C) - cbuf[step, :, 1].reshape(n, C) / growth
        target = new_part + fixed
        for peer in ch_p.peers():
            ch_p.arrived(step, peer, precv.at[step, peer])
        product = precv[step, 0]
        for i in range(1, num_doc):
            product += precv[step, i]
        previous = jnp.zeros((n, C), jnp.float32) if step == 0 else old_product
        residue = target - (product - (previous - product + applied) / growth)
        old_product = product
    for hop in range(1, num_doc):
        for s in range(subs):

            @pl.when(me >= hop)
            def _(hop=hop, s=s):
                w_copy(0, me - hop, s, me).wait_recv()

                @pl.when(me + 1 < num_doc)
                def _():
                    w_copy(0, me - hop, s, me + 1).start()

            @pl.when(me + hop < num_doc)
            def _(hop=hop, s=s):
                w_copy(1, me + hop, s, me).wait_recv()

                @pl.when(me >= 1)
                def _():
                    w_copy(1, me + hop, s, me - 1).start()

    for peer in ch_c.peers():
        ch_c.arrived(ITERS - 1, peer, cbuf.at[ITERS - 1, peer])
    m_ref[...] = cbuf[ITERS - 1, :, 0].reshape(n, C)
    for hop in range(num_doc):
        for s in range(subs):

            @pl.when((me >= hop) & (me + 1 < num_doc))
            def _(hop=hop, s=s):
                w_copy(0, me - hop, s, me + 1).wait_send()

            @pl.when((me + hop < num_doc) & (me >= 1))
            def _(hop=hop, s=s):
                w_copy(1, me + hop, s, me - 1).wait_send()

    for channel in (ch_s, ch_y, ch_c, ch_p, ch_1, ch_2):
        channel.drain()


def per_device(documents, directions, phase, amplitude, doc_weight, labels):
    n, local_inputs = documents.shape
    input_rows, width_tile = directions.shape
    num_feat = lax.axis_size("feat")
    num_doc = lax.axis_size("doc")
    chunk = width_tile // num_doc
    subs = max(1, min(4, chunk // 128))
    share = n // num_feat
    f32, bf16 = jnp.float32, jnp.bfloat16
    vmem = pl.BlockSpec(memory_space=pltpu.VMEM)
    dma = pltpu.SemaphoreType.DMA
    shape = jax.ShapeDtypeStruct
    features, features_t, gram = pl.pallas_call(
        functools.partial(build_kernel, num_doc, num_feat, subs, (2.0 / width_tile) ** 0.5),
        out_shape=(
            shape((num_doc * n, chunk), f32),
            shape((chunk, num_doc * n), f32),
            shape((n, n), f32),
        ),
        in_specs=[vmem, pl.BlockSpec(memory_space=pl.ANY), vmem, vmem],
        out_specs=(vmem, vmem, vmem),
        scratch_shapes=[
            pltpu.VMEM((num_feat, n, local_inputs), bf16),
            pltpu.VMEM((num_doc, n, num_feat * local_inputs), bf16),
            pltpu.VMEM((num_doc, input_rows, chunk), bf16),
            pltpu.VMEM((num_doc, n, n), f32),
            pltpu.VMEM((num_doc, n, n), f32),
            dma((2, 1, num_feat)),
            dma((2, 1, num_doc)),
            dma((2, subs, num_doc)),
            dma((2, 1, num_doc)),
            dma,
        ],
        compiler_params=pltpu.CompilerParams(
            collective_id=0, has_side_effects=True, vmem_limit_bytes=48 * 1024 * 1024
        ),
        name="build",
    )(
        documents,
        directions,
        phase.reshape(num_doc, 1, chunk),
        amplitude.reshape(num_doc, 1, chunk),
    )
    eye = jnp.eye(n, dtype=f32)
    factor = jnp.linalg.cholesky(gram)
    lower_inv = lax.linalg.triangular_solve(factor, eye, left_side=True, lower=True)
    inverse = lax.dot_general(lower_inv, lower_inv, (((0,), (0,)), ((), ())), precision=HI)
    rounds = ITERS - 1
    return pl.pallas_call(
        functools.partial(admm_kernel, num_doc, num_feat, subs),
        out_shape=(shape((n, C), f32), shape((width_tile, C), f32)),
        in_specs=[vmem] * 5,
        out_specs=(vmem, vmem),
        scratch_shapes=[
            pltpu.VMEM((ITERS, num_doc, n, C), f32),
            pltpu.VMEM((ITERS, n, C), f32),
            pltpu.VMEM((ITERS, num_feat, share, C), f32),
            pltpu.VMEM((ITERS, num_feat, 2, share, C), f32),
            pltpu.VMEM((rounds, num_doc, n, C), f32),
            pltpu.VMEM((rounds, num_doc, n, C), f32),
            pltpu.VMEM((rounds, num_doc, 2, 8, C), f32),
            pltpu.VMEM((rounds, num_feat, 2, 8, C), f32),
            pltpu.VMEM((chunk, C), f32),
            pltpu.VMEM((chunk, C), f32),
            pltpu.VMEM((chunk, C), f32),
            dma((2, ITERS, num_doc)),
            dma((2, ITERS, num_feat)),
            dma((2, ITERS, num_feat)),
            dma((2, rounds, num_doc)),
            dma((2, rounds, num_doc)),
            dma((2, rounds, num_feat)),
            dma((2, 2, num_doc, subs)),
        ],
        compiler_params=pltpu.CompilerParams(
            collective_id=1, has_side_effects=True, vmem_limit_bytes=48 * 1024 * 1024
        ),
        name="admm",
    )(features, features_t, inverse, labels[:, None], doc_weight[:, None])


def solution(mesh):
    in_specs = (P("doc", "feat"), P("doc", "feat"), P("feat"), P("feat"), P("doc"), P("doc"))
    out_specs = (P("doc", None), P("feat", None))
    return jax.shard_map(
        per_device, mesh=mesh, in_specs=in_specs, out_specs=out_specs, check_vma=False
    )
```

time: 667 us -> 167 us (0.25); the launches traced: 657 us -> 167 us
  waiting for transfers between devices: 413 us -> 0 us
  Pallas kernels: 0 us -> 134 us
  blocking collectives: 128 us -> 0 us
  matrix products: 49.5 us -> 0.54 us
  between operations: 22.1 us -> 0.71 us
  other arithmetic: 40.1 us -> 22.9 us
    psum x3 -> x0, waiting for transfers between devices: 253 us -> none  [per_device(): summed = lax.psum(new_copy + duals_x, 'doc')]
    pallas_call x0 -> x2, Pallas kernels: none -> 134 us  [the longest x1 82.7 us: per_device(): pl.pallas_call(functools.partial(admm_kernel, num_doc, num_feat, subs), o...]
    reduce_scatter x3 -> x0, waiting for transfers between devices: 95.1 us -> none  [per_device(): lax.psum_scatter(partial_value, 'feat', scatter_dimension=0, tiled=True)]
    psum x2 -> x0, blocking collectives: 78.6 us -> none  [per_device(): lax.psum((jnp.sum((new_copy - weights) ** 2) + margin_gap, jnp.sum((weigh...]
    all_gather x1 -> x0, waiting for transfers between devices: 62.9 us -> none  [per_device(): lax.all_gather(directions, 'doc', axis=0, tiled=True)]
    all_gather x5 -> x0, blocking collectives: 49.8 us -> none  [the longest x3 31.4 us: per_device(): correction = lax.all_gather(correction, 'feat', axis=0, tiled=True)]
    dot_general x11 -> x1, matrix products: 48 us -> 0.29 us  [per_device(): lax.dot_general(lower_inv, lower_inv, (((0,), (0,)), ((), ())), precision...]
    reduce_sum x5 -> x0, other arithmetic: 12.1 us -> none  [the longest x2 7.78 us: per_device(): jnp.sum((weights - old_weights) ** 2) + margin_move]
  transfers between devices with their start and end apart: 7 -> 0, of which waited for: 7 -> 0; matrix products, arithmetic and copies ran while one was open for 1% -> 0% of each run, Pallas kernels for 0% -> 0%
where the time goes in v2:
time: 167 us
  Pallas kernels  134 us (80%)
  other arithmetic  22.9 us (14%)
  local copies, waits for them, and re-layouts  8.36 us (5%)
    pallas_call x1, Pallas kernels, per_device(): pl.pallas_call(functools.partial(admm_kernel, num_doc, num_feat, subs), o...  82.7 us
    pallas_call x1, Pallas kernels, per_device(): pl.pallas_call(functools.partial(build_kernel, num_doc, num_feat, subs, (...  51.7 us
    another operation x3, other arithmetic, per_device(): factor = jnp.linalg.cholesky(gram)  12.4 us
    another operation x2, other arithmetic, per_device(): lax.linalg.triangular_solve(factor, eye, left_side=True, lower=True)  10.5 us
    unnamed x11, local copies, waits for them, and re-layouts  6.74 us

profile of v2, /device:TPU:0, one launch (start us, length us, event | category | flops | bytes accessed | tf_op | source)
XLA Modules:
  0.0 166.9 jit_solution(16688060040071727035)
XLA Ops:
  0.6 0.8 copy.8.docs_ref
  1.5 0.8 copy.11.dw_ref
  2.2 0.8 copy.10.lab_ref
  3.0 0.0 copy-start.1
  3.0 1.2 copy-done.1
  4.2 0.0 copy-start.2
  4.2 0.7 copy-done.2
  4.9 0.0 copy-start.3
  4.9 0.7 copy-done.3
  5.6 51.7 %build.1 = (f32[512,1024]{1,0:T(8,128)S(1)}, f32[1024,512]{1,0:T(8,128)S(1)}, f32[128,128]{1,0:T(8,128)S(1)}) custom-call(bf16[128,64]{1,0:T(8,128)(2,1)S(1)} %copy.8.docs_ref, bf16[128,4096]{1,0:T(8,128)(2,1)S(1)} %copy-done.1, f32[4,1,1024]{2,1,0:T(1,128)S(1)} %bitcast.15, f32[4,1,1024]{2,1,0:T(1,128)S(1)} %bitcast.16), custom_call_target="tpu_custom_call" | custom-call | tf_op jit(solution)/shard_map/build/pallas_call | solution.py:390
  57.4 0.0 copy-start
  57.4 1.3 copy-done
  58.7 0.1 copy.9
  58.8 11.7 %cholesky.17 = f32[128,128]{1,0:T(8,128)S(1)} custom-call(f32[128,128]{1,0:T(8,128)S(1)} %fusion.3), custom_call_target="Cholesky" | custom-call | tf_op jit(solution)/shard_map/jit(cholesky)/cholesky | solution.py:422
  70.6 0.6 compare_reduce_fusion
  71.2 0.7 fusion
  71.9 9.8 %custom-call.6 = f32[1,128,128]{1,2,0:T(8,128)S(1)} custom-call(f32[1,128,128]{2,1,0:T(8,128)S(1)} %fusion), custom_call_target="InvertDiagBlocksLowerTriangular" | custom-call | tf_op jit(solution)/shard_map/triangular_solve | solution.py:423
  81.7 0.2 fusion.1
  81.9 0.3 fusion.4.inv_ref
  82.2 82.7 %admm.1 = (f32[128,128]{1,0:T(8,128)S(1)}, f32[4096,128]{1,0:T(8,128)S(1)}) custom-call(f32[512,1024]{1,0:T(8,128)S(1)} %get-tuple-element.5.feat_ref, f32[1024,512]{1,0:T(8,128)} %copy-done, f32[128,128]{1,0:T(8,128)S(1)} %fusion.4.inv_ref, s32[128,1]{1,0:T(8,128)S(1)} %copy.10.lab_ref, f32[128,1]{1,0:T(8,128)S(1)} %copy.11.dw_ref), custom_call_target="tpu_custom_call" | custom-call | tf_op jit(solution)/shard_map/admm/pallas_call | solution.py:426
  164.9 0.6 copy.14
  165.5 1.3 copy.15
  (2 shorter events, 0.0 us)
Async XLA Ops:
  3.0 1.2 copy-start.1
  4.2 0.7 copy-start.2
  4.9 0.7 copy-start.3
  57.4 1.3 copy-start

commit v3 on v2

--- a/solution.py
+++ b/solution.py
@@ -47,6 +47,17 @@
     return poly * (1.0 - 2.0 * odd)
 
 
+def split(values):
+    high = values.astype(jnp.bfloat16)
+    return high, (values - high.astype(jnp.float32)).astype(jnp.bfloat16)
+
+
+def split_dot(high, low, pair):
+    both = jnp.dot(high, pair, preferred_element_type=jnp.float32)
+    rest = jnp.dot(low, pair[:, :C], preferred_element_type=jnp.float32)
+    return both[:, :C] + (both[:, C:] + rest)
+
+
 def remote(src, dst, send_sem, recv_sem, axis, peer):
     return pltpu.make_async_remote_copy(
         src_ref=src,
@@ -97,9 +108,10 @@
 
 def build_kernel(
     num_doc, num_feat, subs, scale,
-    docs_ref, dir_ref, phase_ref, amp_ref,
+    docs_ref, dir_ref, phase_hbm, amp_hbm,
     feat_ref, featt_ref, gram_ref,
-    dpart, drow, dirs, gsend, grecv, part_sems, row_sems, dir_sems, gram_sems, local_sem,
+    dpart, phase_ref, amp_ref, dirs, gsend, grecv,
+    part_sems, row_sems, dir_sems, gram_sems, local_sem, table_sems,
 ):
     n = docs_ref.shape[0]
     chunk = dirs.shape[2]
@@ -111,8 +123,14 @@
     ch_row = Channel(row_sems, "doc", num_doc)
     ch_dir = Channel(dir_sems, "doc", num_doc)
     ch_gram = Channel(gram_sems, "doc", num_doc)
-    for peer in ch_part.peers():
-        ch_part.send(0, peer, docs_ref, dpart.at[fme])
+    for peer in ch_row.peers():
+        ch_row.send(0, peer, docs_ref, dpart.at[fme, me])
+    tables = [
+        pltpu.make_async_copy(phase_hbm.at[me], phase_ref, table_sems.at[0]),
+        pltpu.make_async_copy(amp_hbm.at[me], amp_ref, table_sems.at[1]),
+    ]
+    for table in tables:
+        table.start()
     local = pltpu.make_async_copy(
         dir_ref.at[:, pl.ds(pl.multiple_of(me * chunk, chunk), chunk)], dirs.at[me], local_sem
     )
@@ -123,21 +141,25 @@
             ch_dir.send(
                 s, peer, dir_ref.at[:, cols], dirs.at[me, :, pl.ds(s * wide, wide)]
             )
-    dpart[fme] = docs_ref[...]
+    dpart[fme, me] = docs_ref[...]
+    for peer in ch_row.peers():
+        ch_row.arrived(0, peer, dpart.at[fme, peer])
+    for peer in ch_part.peers():
+        ch_part.send(0, peer, dpart.at[fme], dpart.at[fme])
     for peer in ch_part.peers():
         ch_part.arrived(0, peer, dpart.at[peer])
-    row = jnp.concatenate(
-        [dpart[k].astype(jnp.float32) for k in range(num_feat)], axis=1
+    full = jnp.concatenate(
+        [
+            dpart[k].reshape(num_doc * n, docs_ref.shape[1]).astype(jnp.float32)
+            for k in range(num_feat)
+        ],
+        axis=1,
     ).astype(jnp.bfloat16)
-    drow[me] = row
-    for peer in ch_row.peers():
-        ch_row.send(0, peer, drow.at[me], drow.at[me])
-    for peer in ch_row.peers():
-        ch_row.arrived(0, peer, drow.at[peer])
     local.wait()
-    full = drow[...].reshape(num_doc * n, drow.shape[2])
-    phase = phase_ref[me]
-    amp = scale * amp_ref[me]
+    for table in tables:
+        table.wait()
+    phase = phase_ref[...]
+    amp = scale * amp_ref[...]
     for s in range(subs):
         cols = slice(s * wide, (s + 1) * wide)
         for peer in ch_dir.peers():
@@ -145,8 +167,9 @@
         piece = dirs[:, :, cols].reshape(full.shape[1], wide)
         angles = jnp.dot(full, piece, preferred_element_type=jnp.float32)
         feats = amp[:, cols] * cosine(angles + phase[:, cols])
-        feat_ref[:, cols] = feats
-        featt_ref[cols, :] = feats.T
+        flipped = feats.T
+        feat_ref[0, :, cols], feat_ref[1, :, cols] = split(feats)
+        featt_ref[0, cols, :], featt_ref[1, cols, :] = split(flipped)
         for i in range(num_doc):
             block = feats[i * n : (i + 1) * n]
             term = lax.dot_general(block, block, (((1,), (1,)), ((), ())), precision=HI)
@@ -169,6 +192,21 @@
         channel.drain()
 
 
+def sweep_kernel(gram_ref, inverse_ref):
+    values = gram_ref[...]
+    n = values.shape[0]
+    lanes = lax.broadcasted_iota(jnp.int32, (1, n), 1)
+    rows = lax.broadcasted_iota(jnp.int32, (n, 1), 0)
+    for k in range(n):
+        pivot = 1.0 / values[k : k + 1, k : k + 1]
+        row = jnp.where(lanes == k, pivot, values[k : k + 1, :] * pivot)
+        column = values[:, k : k + 1]
+        values = jnp.where(
+            rows == k, row, jnp.where(lanes == k, 0.0, values) - column * row
+        )
+    inverse_ref[...] = values
+
+
 def fold(values):
     return jnp.sum(values.reshape(values.shape[0] // 8, 8, values.shape[1]), axis=0)
 
@@ -181,7 +219,7 @@
     num_doc, num_feat, subs,
     feat_ref, featt_ref, inv_ref, lab_ref, dw_ref,
     m_ref, w_ref,
-    solved, part, yrecv, cbuf, psend, precv, sc1, sc2, z, lastmove, lastlift,
+    solved, part, yrecv, cbuf, psend, precv, sc1, sc2, z, lastmove, lastlift, signs_ref, weight_ref,
     s_sems, y_sems, c_sems, p_sems, sc1_sems, sc2_sems, w_sems,
 ):
     n = inv_ref.shape[0]
@@ -197,14 +235,16 @@
     ch_p = Channel(p_sems, "doc", num_doc)
     ch_1 = Channel(sc1_sems, "doc", num_doc)
     ch_2 = Channel(sc2_sems, "feat", num_feat)
-    classes = lax.broadcasted_iota(jnp.int32, (n, C), 1)
-    all_signs = jnp.where(lab_ref[...] == classes, 1.0, -1.0)
-    start = logistic_prox(jnp.zeros((n, C), jnp.float32), all_signs, dw_ref[...])
+    classes = lax.broadcasted_iota(jnp.int32, (n, C), 1).astype(jnp.float32)
+    spread = jnp.broadcast_to(lab_ref[...].astype(jnp.float32), (C, n)).T
+    all_weight = jnp.broadcast_to(dw_ref[...], (C, n)).T
+    all_signs = jnp.where(spread == classes, 1.0, -1.0)
+    start = logistic_prox(jnp.zeros((n, C), jnp.float32), all_signs, all_weight)
+    signs_ref[...] = all_signs
+    weight_ref[...] = all_weight
     own = pl.ds(pl.multiple_of(fme * share, share), share)
-    signs = jnp.where(
-        lab_ref[own, :] == lax.broadcasted_iota(jnp.int32, (share, C), 1), 1.0, -1.0
-    )
-    weight = dw_ref[own, :]
+    signs = signs_ref[own, :]
+    weight = weight_ref[own, :]
     margins = logistic_prox(jnp.zeros((share, C), jnp.float32), signs, weight)
     duals = jnp.zeros((share, C), jnp.float32)
     rho = jnp.ones((1, 1), jnp.float32)
@@ -249,7 +289,7 @@
             ch_c.send(step, peer, cbuf.at[step, fme], cbuf.at[step, fme])
         for peer in ch_s.peers():
             ch_s.arrived(step, peer, solved.at[step, peer])
-        everything = solved[step].reshape(num_doc * n, C)
+        everything = jnp.concatenate(split(solved[step].reshape(num_doc * n, C)), axis=1)
         limit = shrink_level / (rho * num_doc)
         if not last:
             gap = fold((sums - margins) ** 2) if share > 8 else (sums - margins) ** 2
@@ -265,7 +305,7 @@
             dual = shift
         for s in range(subs):
             rows = slice(s * wide, (s + 1) * wide)
-            lift = jnp.dot(featt_ref[rows, :], everything, precision=HI)
+            lift = split_dot(featt_ref[0, rows, :], featt_ref[1, rows, :], everything)
             if step == 0:
                 fresh = shrink_values(lift / num_doc, limit)
                 move = -fresh
@@ -299,9 +339,10 @@
         sc1[step, me, 1] = dual
         for peer in ch_1.peers():
             ch_1.send(step, peer, sc1.at[step, me], sc1.at[step, me])
-        weights = z[...]
+        weights = jnp.concatenate(split(z[...]), axis=1)
         for i in range(num_doc):
-            psend[step, i] = jnp.dot(feat_ref[i * n : (i + 1) * n, :], weights, precision=HI)
+            block = slice(i * n, (i + 1) * n)
+            psend[step, i] = split_dot(feat_ref[0, block, :], feat_ref[1, block, :], weights)
         for peer in ch_p.peers():
             ch_p.send(step, peer, psend.at[step, peer], precv.at[step, me])
         precv[step, me] = psend[step, me]
@@ -390,15 +431,16 @@
     features, features_t, gram = pl.pallas_call(
         functools.partial(build_kernel, num_doc, num_feat, subs, (2.0 / width_tile) ** 0.5),
         out_shape=(
-            shape((num_doc * n, chunk), f32),
-            shape((chunk, num_doc * n), f32),
+            shape((2, num_doc * n, chunk), bf16),
+            shape((2, chunk, num_doc * n), bf16),
             shape((n, n), f32),
         ),
-        in_specs=[vmem, pl.BlockSpec(memory_space=pl.ANY), vmem, vmem],
+        in_specs=[vmem] + [pl.BlockSpec(memory_space=pl.ANY)] * 3,
         out_specs=(vmem, vmem, vmem),
         scratch_shapes=[
-            pltpu.VMEM((num_feat, n, local_inputs), bf16),
-            pltpu.VMEM((num_doc, n, num_feat * local_inputs), bf16),
+            pltpu.VMEM((num_feat, num_doc, n, local_inputs), bf16),
+            pltpu.VMEM((1, chunk), f32),
+            pltpu.VMEM((1, chunk), f32),
             pltpu.VMEM((num_doc, input_rows, chunk), bf16),
             pltpu.VMEM((num_doc, n, n), f32),
             pltpu.VMEM((num_doc, n, n), f32),
@@ -407,6 +449,7 @@
             dma((2, subs, num_doc)),
             dma((2, 1, num_doc)),
             dma,
+            dma((2,)),
         ],
         compiler_params=pltpu.CompilerParams(
             collective_id=0, has_side_effects=True, vmem_limit_bytes=48 * 1024 * 1024
@@ -418,10 +461,13 @@
         phase.reshape(num_doc, 1, chunk),
         amplitude.reshape(num_doc, 1, chunk),
     )
-    eye = jnp.eye(n, dtype=f32)
-    factor = jnp.linalg.cholesky(gram)
-    lower_inv = lax.linalg.triangular_solve(factor, eye, left_side=True, lower=True)
-    inverse = lax.dot_general(lower_inv, lower_inv, (((0,), (0,)), ((), ())), precision=HI)
+    inverse = pl.pallas_call(
+        sweep_kernel,
+        out_shape=shape((n, n), f32),
+        in_specs=[vmem],
+        out_specs=vmem,
+        name="invert",
+    )(gram)
     rounds = ITERS - 1
     return pl.pallas_call(
         functools.partial(admm_kernel, num_doc, num_feat, subs),
@@ -440,6 +486,8 @@
             pltpu.VMEM((chunk, C), f32),
             pltpu.VMEM((chunk, C), f32),
             pltpu.VMEM((chunk, C), f32),
+            pltpu.VMEM((n, C), f32),
+            pltpu.VMEM((n, C), f32),
             dma((2, ITERS, num_doc)),
             dma((2, ITERS, num_feat)),
             dma((2, ITERS, num_feat)),
@@ -452,7 +500,7 @@
             collective_id=1, has_side_effects=True, vmem_limit_bytes=48 * 1024 * 1024
         ),
         name="admm",
-    )(features, features_t, inverse, labels[:, None], doc_weight[:, None])
+    )(features, features_t, inverse, labels.reshape(1, n), doc_weight.reshape(1, n))
 
 
 def solution(mesh):

time: 167 us -> 145 us (0.87)
  other arithmetic: 22.9 us -> 0 us
    another operation x5 -> x0, other arithmetic: 22.9 us -> none  [the longest x3 12.4 us: per_device(): factor = jnp.linalg.cholesky(gram)]
    pallas_call x0 -> x1, Pallas kernels: none -> 12.5 us  [per_device(): pl.pallas_call(sweep_kernel, out_shape=shape((n, n), f32), in_specs=[vmem...]
    pallas_call x1, Pallas kernels: 51.7 us -> 39.4 us  [per_device(): pl.pallas_call(functools.partial(build_kernel, num_doc, num_feat, subs, (...]
    unnamed x11 -> x19, local copies, waits for them, and re-layouts: 6.74 us -> 9.53 us
where the time goes in v3:
time: 145 us; the launch traced here: 144 us
  Pallas kernels  134 us (92%)
  local copies, waits for them, and re-layouts  9.53 us (7%)
    pallas_call x1, Pallas kernels, per_device(): pl.pallas_call(functools.partial(admm_kernel, num_doc, num_feat, subs), o...  82.4 us
    pallas_call x1, Pallas kernels, per_device(): pl.pallas_call(functools.partial(build_kernel, num_doc, num_feat, subs, (...  39.4 us
    pallas_call x1, Pallas kernels, per_device(): pl.pallas_call(sweep_kernel, out_shape=shape((n, n), f32), in_specs=[vmem...  12.5 us
    unnamed x19, local copies, waits for them, and re-layouts  9.53 us

profile of v3, /device:TPU:0, one launch (start us, length us, event | category | flops | bytes accessed | tf_op | source)
XLA Modules:
  0.0 144.5 jit_solution(866796628512300711)
XLA Ops:
  0.6 0.8 copy.8.docs_ref
  1.5 0.0 copy-start.1
  1.5 1.2 copy-done.1
  2.7 0.0 copy-start.4
  2.7 0.7 copy-done.4
  3.4 0.0 copy-start.5
  3.4 0.7 copy-done.5
  4.1 39.4 %build.1 = (bf16[2,512,1024]{2,1,0:T(8,128)(2,1)S(1)}, bf16[2,1024,512]{2,1,0:T(8,128)(2,1)S(1)}, f32[128,128]{1,0:T(8,128)S(1)}) custom-call(bf16[128,64]{1,0:T(8,128)(2,1)S(1)} %copy.8.docs_ref, bf16[128,4096]{1,0:T(8,128)(2,1)S(1)} %copy-done.1, f32[4,1,1024]{2,1,0:T(1,128)S(1)} %bitcast.4, f32[4,1,1024]{2,1,0:T(1,128)S(1)} %bitcast.5), custom_call_target="tpu_custom_call" | custom-call | tf_op jit(solution)/shard_map/build/pallas_call | solution.py:431
  43.6 0.0 copy-start
  43.6 1.3 copy-done
  44.9 0.0 copy-start.3
  44.9 0.6 copy-done.3
  45.5 12.5 %invert.1.inv_ref = f32[128,128]{1,0:T(8,128)} custom-call(f32[128,128]{1,0:T(8,128)} %copy-done.3), custom_call_target="tpu_custom_call" | custom-call | tf_op jit(solution)/shard_map/invert/pallas_call | solution.py:464
  58.0 0.0 copy-start.2
  58.0 0.8 copy-done.2
  58.8 0.0 copy-start.6
  58.8 0.7 copy-done.6
  59.5 0.0 copy-start.7
  59.5 0.7 copy-done.7
  60.2 82.4 %admm.1 = (f32[128,128]{1,0:T(8,128)S(1)}, f32[4096,128]{1,0:T(8,128)S(1)}) custom-call(bf16[2,512,1024]{2,1,0:T(8,128)(2,1)S(1)} %get-tuple-element.5.feat_ref, bf16[2,1024,512]{2,1,0:T(8,128)(2,1)} %copy-done, f32[128,128]{1,0:T(8,128)S(1)} %copy-done.2, s32[1,128]{1,0:T(1,128)S(1)} %bitcast.6, f32[1,128]{1,0:T(1,128)S(1)} %bitcast.7), custom_call_target="tpu_custom_call" | custom-call | tf_op jit(solution)/shard_map/admm/pallas_call | solution.py:472
  142.5 0.6 copy.11
  143.2 1.3 copy.12
Async XLA Ops:
  1.5 1.2 copy-start.1
  2.7 0.7 copy-start.4
  3.4 0.7 copy-start.5
  43.6 1.3 copy-start
  44.9 0.6 copy-start.3
  58.0 0.8 copy-start.2
  58.8 0.7 copy-start.6
  59.5 0.7 copy-start.7

commit v4 on v3

--- a/solution.py
+++ b/solution.py
@@ -228,7 +228,6 @@
     wide = chunk // subs
     me = lax.axis_index("doc")
     fme = lax.axis_index("feat")
-    greet(num_doc, num_feat)
     ch_s = Channel(s_sems, "doc", num_doc)
     ch_y = Channel(y_sems, "feat", num_feat)
     ch_c = Channel(c_sems, "feat", num_feat)
@@ -416,6 +415,24 @@
         channel.drain()
 
 
+def whole_kernel(
+    num_doc, num_feat, subs, scale,
+    docs_ref, dir_ref, phase_hbm, amp_hbm, lab_ref, dw_ref,
+    m_ref, w_ref,
+    feat_ref, featt_ref, gram_ref, inv_ref,
+    *scratch,
+):
+    build_kernel(
+        num_doc, num_feat, subs, scale,
+        docs_ref, dir_ref, phase_hbm, amp_hbm, feat_ref, featt_ref, gram_ref, *scratch[:12],
+    )
+    sweep_kernel(gram_ref, inv_ref)
+    admm_kernel(
+        num_doc, num_feat, subs,
+        feat_ref, featt_ref, inv_ref, lab_ref, dw_ref, m_ref, w_ref, *scratch[12:],
+    )
+
+
 def per_device(documents, directions, phase, amplitude, doc_weight, labels):
     n, local_inputs = documents.shape
     input_rows, width_tile = directions.shape
@@ -428,16 +445,20 @@
     vmem = pl.BlockSpec(memory_space=pltpu.VMEM)
     dma = pltpu.SemaphoreType.DMA
     shape = jax.ShapeDtypeStruct
-    features, features_t, gram = pl.pallas_call(
-        functools.partial(build_kernel, num_doc, num_feat, subs, (2.0 / width_tile) ** 0.5),
-        out_shape=(
-            shape((2, num_doc * n, chunk), bf16),
-            shape((2, chunk, num_doc * n), bf16),
-            shape((n, n), f32),
+    rounds = ITERS - 1
+    any_space = pl.BlockSpec(memory_space=pl.ANY)
+    return pl.pallas_call(
+        functools.partial(
+            whole_kernel, num_doc, num_feat, subs, (2.0 / width_tile) ** 0.5
         ),
-        in_specs=[vmem] + [pl.BlockSpec(memory_space=pl.ANY)] * 3,
-        out_specs=(vmem, vmem, vmem),
+        out_shape=(shape((n, C), f32), shape((width_tile, C), f32)),
+        in_specs=[vmem, any_space, any_space, any_space, vmem, vmem],
+        out_specs=(vmem, vmem),
         scratch_shapes=[
+            pltpu.VMEM((2, num_doc * n, chunk), bf16),
+            pltpu.VMEM((2, chunk, num_doc * n), bf16),
+            pltpu.VMEM((n, n), f32),
+            pltpu.VMEM((n, n), f32),
             pltpu.VMEM((num_feat, num_doc, n, local_inputs), bf16),
             pltpu.VMEM((1, chunk), f32),
             pltpu.VMEM((1, chunk), f32),
@@ -450,31 +471,6 @@
             dma((2, 1, num_doc)),
             dma,
             dma((2,)),
-        ],
-        compiler_params=pltpu.CompilerParams(
-            collective_id=0, has_side_effects=True, vmem_limit_bytes=48 * 1024 * 1024
-        ),
-        name="build",
-    )(
-        documents,
-        directions,
-        phase.reshape(num_doc, 1, chunk),
-        amplitude.reshape(num_doc, 1, chunk),
-    )
-    inverse = pl.pallas_call(
-        sweep_kernel,
-        out_shape=shape((n, n), f32),
-        in_specs=[vmem],
-        out_specs=vmem,
-        name="invert",
-    )(gram)
-    rounds = ITERS - 1
-    return pl.pallas_call(
-        functools.partial(admm_kernel, num_doc, num_feat, subs),
-        out_shape=(shape((n, C), f32), shape((width_tile, C), f32)),
-        in_specs=[vmem] * 5,
-        out_specs=(vmem, vmem),
-        scratch_shapes=[
             pltpu.VMEM((ITERS, num_doc, n, C), f32),
             pltpu.VMEM((ITERS, n, C), f32),
             pltpu.VMEM((ITERS, num_feat, share, C), f32),
@@ -497,10 +493,17 @@
             dma((2, 2, num_doc, subs)),
         ],
         compiler_params=pltpu.CompilerParams(
-            collective_id=1, has_side_effects=True, vmem_limit_bytes=48 * 1024 * 1024
+            collective_id=0, has_side_effects=True, vmem_limit_bytes=48 * 1024 * 1024
         ),
         name="admm",
-    )(features, features_t, inverse, labels.reshape(1, n), doc_weight.reshape(1, n))
+    )(
+        documents,
+        directions,
+        phase.reshape(num_doc, 1, chunk),
+        amplitude.reshape(num_doc, 1, chunk),
+        labels.reshape(1, n),
+        doc_weight.reshape(1, n),
+    )
 
 
 def solution(mesh):

time: 145 us -> 137 us (0.945)
  Pallas kernels: 134 us -> 129 us
  local copies, waits for them, and re-layouts: 9.53 us -> 6.75 us
    pallas_call x3 -> x1, Pallas kernels: 134 us -> 129 us  [per_device(): pl.pallas_call(functools.partial(whole_kernel, num_doc, num_feat, subs, (...]
    unnamed x19 -> x13, local copies, waits for them, and re-layouts: 9.53 us -> 6.75 us
where the time goes in v4:
time: 137 us; the launch traced here: 136 us
  Pallas kernels  129 us (94%)
  local copies, waits for them, and re-layouts  6.75 us (5%)
    pallas_call x1, Pallas kernels, per_device(): pl.pallas_call(functools.partial(whole_kernel, num_doc, num_feat, subs, (...  129 us
    unnamed x13, local copies, waits for them, and re-layouts  6.75 us

profile of v4, /device:TPU:0, one launch (start us, length us, event | category | flops | bytes accessed | tf_op | source)
XLA Modules:
  0.0 136.5 jit_solution(273505746778143937)
XLA Ops:
  0.6 0.8 copy.8.docs_ref
  1.5 0.0 copy-start
  1.5 1.2 copy-done
  2.7 0.0 copy-start.1
  2.7 0.7 copy-done.1
  3.4 0.0 copy-start.2
  3.4 0.7 copy-done.2
  4.1 0.0 copy-start.3
  4.1 0.7 copy-done.3
  4.8 0.0 copy-start.4
  4.8 0.7 copy-done.4
  5.4 129.1 %admm.1 = (f32[128,128]{1,0:T(8,128)S(1)}, f32[4096,128]{1,0:T(8,128)S(1)}) custom-call(bf16[128,64]{1,0:T(8,128)(2,1)S(1)} %copy.8.docs_ref, bf16[128,4096]{1,0:T(8,128)(2,1)S(1)} %copy-done, f32[4,1,1024]{2,1,0:T(1,128)S(1)} %bitcast.4, f32[4,1,1024]{2,1,0:T(1,128)S(1)} %bitcast.5, s32[1,128]{1,0:T(1,128)S(1)} %bitcast.6, f32[1,128]{1,0:T(1,128)S(1)} %bitcast.7), custom_call_target="tpu_custom_call" | custom-call | tf_op jit(solution)/shard_map/admm/pallas_call | solution.py:450
  134.5 0.6 copy.11
  135.1 1.3 copy.12
Async XLA Ops:
  1.5 1.2 copy-start
  2.7 0.7 copy-start.1
  3.4 0.7 copy-start.2
  4.1 0.7 copy-start.3
  4.8 0.7 copy-start.4
